TPU v7x, 512 devices: a whole 4x8x8 slice. The times are simulated.
512 devices in a mesh: sec: 2 (over core), ctx: 64 (over x, z_hi, y), head: 4 (over z_lo).
Axes of the slice: x: 4, y: 8, z: 8 (z_hi: 2, z_lo: 4; z = z_hi * 4 + z_lo), core: 2. Of those that a mesh axis runs over, the one named last changes fastest.
Arguments:
- query_self: bfloat16 [12288, 2048], P('ctx', ('sec', 'head')), may hold values from -12 to 12
- key_self: bfloat16 [12288, 2048], P('ctx', ('sec', 'head')), may hold values from -6 to 6
- value_self: bfloat16 [12288, 2048], P('ctx', ('sec', 'head')), may hold values from -6 to 6
- query_cross: bfloat16 [12288, 2048], P('ctx', ('sec', 'head')), may hold values from -12 to 12
- neighbour_kv: bfloat16 [512, 128, 4096], P(('sec', 'ctx', 'head')), may hold values from -6 to 6
- neighbour_map: int32 [192, 2], P('ctx'), may hold values from 0 to 7, all different within a row
Outputs:
- self_out: bfloat16 [12288, 2048], P('ctx', ('sec', 'head'))
- cross_out: bfloat16 [12288, 2048], P('ctx', ('sec', 'head'))
Inputs may be any that keep to these rules, and one draw needn't show every extreme that they name: `neighbour_map`: entry v of stretch c names slot v % 1 of the device at index v // 1 along sec+head that shares stretch c's context shard; a stretch's two entries differ.
All inputs are finite; a program needn't handle non-finite values.
Results may differ from a plain program's by a relative error of at most 0.0035.
Values may be sent and summed in bfloat16 or wider, within the bound.
No kernel may reach another device: no remote copies, remote signals or barrier semaphores. Data moves between devices by JAX's collectives and lax.ppermute only.
A program may use at most 64 MiB of HBM per device.

v0:
```python
import math
import jax
import jax.numpy as jnp
from jax import lax
from jax.sharding import PartitionSpec as P

HD = 128
STRETCH = 64
MASKED_SCORE = -1e30


def attend_block(carried, queries, key_block, value_block, key_mask, score_scale):
    row_top, row_total, summed = carried
    scores = (
        jnp.einsum("qhd,khd->hqk", queries, key_block, preferred_element_type=jnp.float32)
        * score_scale
    )
    masked = jnp.where(key_mask, scores, MASKED_SCORE)
    new_top = jnp.maximum(row_top, jnp.max(masked, axis=-1))
    exp_scores = jnp.where(key_mask, jnp.exp(masked - new_top[:, :, None]), 0.0)
    factor = jnp.exp(row_top - new_top)
    row_total = row_total * factor + jnp.sum(exp_scores, axis=-1)
    update = jnp.einsum(
        "hqk,khd->qhd",
        exp_scores.astype(jnp.bfloat16),
        value_block,
        preferred_element_type=jnp.float32,
    )
    summed = summed * jnp.transpose(factor)[:, :, None] + update
    return (new_top, row_total, summed)


def attend_keys(carried, queries, key_rows, value_rows, positions, score_scale):
    key_count = key_rows.shape[0]
    head_count = queries.shape[1]
    block_rows = math.gcd(key_count, 1024)
    blocks = key_count // block_rows
    key_stack = key_rows.reshape(blocks, block_rows, head_count, HD)
    value_stack = value_rows.reshape(blocks, block_rows, head_count, HD)

    def fold_step(state_now, scanned):
        number, key_block, value_block = scanned
        places = number * block_rows + jnp.arange(block_rows, dtype=jnp.int32)
        key_mask = (places[None, None, :] <= positions[None, :, None]) & (
            places[None, None, :] >= 0
        )
        return (
            attend_block(state_now, queries, key_block, value_block, key_mask, score_scale),
            None,
        )

    carried, _ = lax.scan(
        fold_step, carried, (jnp.arange(blocks, dtype=jnp.int32), key_stack, value_stack)
    )
    return carried


def self_attention(query_self, key_self, value_self, score_scale):
    local_rows, local_width = query_self.shape
    head_count = local_width // HD
    queries = query_self.reshape(local_rows, head_count, HD)
    first_row = lax.axis_index("ctx") * local_rows
    positions = first_row + jnp.arange(local_rows, dtype=jnp.int32)
    carried = (
        jnp.full((head_count, local_rows), MASKED_SCORE, jnp.float32),
        jnp.zeros((head_count, local_rows), jnp.float32),
        jnp.zeros((local_rows, head_count, HD), jnp.float32),
    )
    carried = attend_keys(
        carried,
        queries,
        lax.all_gather(key_self, "ctx", axis=0, tiled=True),
        lax.all_gather(value_self, "ctx", axis=0, tiled=True),
        positions,
        score_scale,
    )
    row_top, row_total, summed = carried
    attended = summed / jnp.transpose(row_total)[:, :, None]
    return attended.reshape(local_rows, local_width).astype(jnp.bfloat16)


def cross_attention(query_cross, neighbour_kv, neighbour_map, score_scale):
    local_rows, local_width = query_cross.shape
    head_count = local_width // HD
    stretch_count = local_rows // STRETCH
    slot_count, block_len, features = neighbour_kv.shape
    group_count = features // (2 * local_width)
    stretch_first = lax.axis_index("ctx") * stretch_count
    keep_stretch = stretch_first + jnp.arange(stretch_count, dtype=jnp.int32) > 0
    parted = neighbour_kv.reshape(slot_count, block_len, group_count, 2 * local_width)
    received = lax.all_to_all(parted, ("sec", "head"), split_axis=2, concat_axis=0, tiled=True)
    received = received.reshape(group_count * slot_count, block_len, 2, head_count, HD)
    chosen = received[neighbour_map]
    chosen = chosen.reshape(stretch_count, neighbour_map.shape[1] * block_len, 2, head_count, HD)
    stretch_queries = query_cross.reshape(stretch_count, STRETCH, head_count, HD)
    scores = (
        jnp.einsum(
            "cqhd,ckhd->chqk", stretch_queries, chosen[:, :, 0], preferred_element_type=jnp.float32
        )
        * score_scale
    )
    row_top = jnp.max(scores, axis=-1, keepdims=True)
    exp_scores = jnp.exp(scores - row_top)
    row_total = jnp.sum(exp_scores, axis=-1)
    summed = jnp.einsum(
        "chqk,ckhd->cqhd",
        exp_scores.astype(jnp.bfloat16),
        chosen[:, :, 1],
        preferred_element_type=jnp.float32,
    )
    attended = summed / jnp.transpose(row_total, (0, 2, 1))[:, :, :, None]
    attended = attended.reshape(local_rows, local_width)
    keep_rows = jnp.repeat(keep_stretch, STRETCH)
    return jnp.where(keep_rows[:, None], attended, 0.0).astype(jnp.bfloat16)


def on_device(query_self, key_self, value_self, query_cross, neighbour_kv, neighbour_map):
    score_scale = 1.0 / math.sqrt(HD)
    self_out = self_attention(query_self, key_self, value_self, score_scale)
    cross_out = cross_attention(query_cross, neighbour_kv, neighbour_map, score_scale)
    return (self_out, cross_out)


def solution(mesh):
    return jax.shard_map(
        on_device,
        mesh=mesh,
        in_specs=(
            P("ctx", ("sec", "head")),
            P("ctx", ("sec", "head")),
            P("ctx", ("sec", "head")),
            P("ctx", ("sec", "head")),
            P(("sec", "ctx", "head"), None, None),
            P("ctx", None),
        ),
        out_specs=(P("ctx", ("sec", "head")), P("ctx", ("sec", "head"))),
        check_vma=False,
    )
```

profile of v0, /device:TPU:4, one launch (start us, length us, event | category | flops | bytes accessed | tf_op | source)
XLA Modules:
  0.0 453.8 jit_solution(10406228715060818741)
XLA Ops:
  7.2 0.7 all-gather.3.cloned.1.call-update
  8.0 0.7 all-gather.5.cloned.1.call-update
  8.7 2.3 copy.37
  10.9 7.4 %all-to-all-start = ((bf16[1,128,8,512]{1,3,0,2:T(8,128)(2,1)}), bf16[1,128,8,512]{1,3,0,2:T(8,128)(2,1)S(1)}, u32[]{:S(2)}, u32[]{:S(2)}) async-start(bf16[1,128,8,512]{1,3,0,2:T(8,128)(2,1)} %bitcast.1), calls=%async_computation | async-start | bytes 2097152 | tf_op jit(solution)/shard_map/all_to_all | solution.py:91
  18.8 26.6 %all-to-all-done = bf16[1,128,8,512]{1,3,0,2:T(8,128)(2,1)S(1)} async-done(((bf16[1,128,8,512]{1,3,0,2:T(8,128)(2,1)}), bf16[1,128,8,512]{1,3,0,2:T(8,128)(2,1)S(1)}, u32[]{:S(2)}, u32[]{:S(2)}) %all-to-all-start) | async-done | bytes 1048608 | tf_op jit(solution)/shard_map/all_to_all | solution.py:91
  45.4 0.7 copy.39
  46.1 0.7 gather_fusion
  47.9 0.7 fusion.18
  48.6 150.6 %all-gather.3.cloned.1.call-done = bf16[12288,256]{1,0:T(8,128)(2,1)} async-done(((bf16[192,256]{1,0:T(8,128)(2,1)}), bf16[12288,256]{1,0:T(8,128)(2,1)}) %all-gather.3.cloned.1.call-update) | async-done | bytes 6291472 | tf_op jit(solution)/shard_map/all_gather | solution.py:72
  199.2 9.7 %reshape.96 = bf16[12,1024,2,128]{3,2,1,0:T(2,128)(2,1)} reshape(bf16[12288,256]{1,0:T(8,128)(2,1)} %all-gather.3.cloned.1.call-done) | data formatting | bytes 12582912 | tf_op jit(solution)/shard_map/reshape | solution.py:38
  208.8 167.1 %all-gather.5.cloned.1.call-done = bf16[12288,256]{1,0:T(8,128)(2,1)} async-done(((bf16[192,256]{1,0:T(8,128)(2,1)}), bf16[12288,256]{1,0:T(8,128)(2,1)}) %all-gather.5.cloned.1.call-update) | async-done | bytes 6291472 | tf_op jit(solution)/shard_map/all_gather | solution.py:73
  375.9 9.7 %reshape.98 = bf16[12,1024,2,128]{3,2,1,0:T(2,128)(2,1)} reshape(bf16[12288,256]{1,0:T(8,128)(2,1)} %all-gather.5.cloned.1.call-done) | data formatting | bytes 12582912 | tf_op jit(solution)/shard_map/reshape | solution.py:39
  385.6 60.6 %while.15 = (s32[]{:T(128)}, f32[2,192]{1,0:T(2,128)S(1)}, f32[2,192]{1,0:T(2,128)S(1)}, f32[192,2,128]{2,0,1:T(8,128)S(1)}, s32[12]{0:T(128)S(1)}, /*index=5*/b...) while((s32[]{:T(128)}, f32[2,192]{1,0:T(2,128)S(1)}, ...), condition=%wide.region_3.4_spmd.clone, body=%wide.region_0.3_spmd.clone.sunk | while | flops 205411776 | bytes 9178801 | solution.py:52
  387.0 1.9 constant_dynamic-slice_fusion.3
  389.5 0.6 fusion.42
  392.0 1.9 constant_dynamic-slice_fusion.3
  397.1 1.9 constant_dynamic-slice_fusion.3
  402.1 1.9 constant_dynamic-slice_fusion.3
  404.6 0.6 fusion.42
  407.2 1.9 constant_dynamic-slice_fusion.3
  409.7 0.6 fusion.42
  412.2 1.9 constant_dynamic-slice_fusion.3
  417.3 1.9 constant_dynamic-slice_fusion.3
  422.3 1.9 constant_dynamic-slice_fusion.3
  424.8 0.6 fusion.42
  427.4 1.9 constant_dynamic-slice_fusion.3
  432.4 1.9 constant_dynamic-slice_fusion.3
  437.5 1.9 constant_dynamic-slice_fusion.3
  440.0 0.6 fusion.42
  442.5 1.9 constant_dynamic-slice_fusion.3
  445.0 0.6 fusion.42
  446.2 0.8 copy_bitcast_fusion.8
  (153 shorter events, 27.9 us)
Async XLA Ops:
  7.2 11.6 %copy-start = (bf16[192,256]{1,0:T(8,128)(2,1)S(1)}, bf16[192,256]{1,0:T(8,128)(2,1)}, u32[]{:S(2)}) copy-start(bf16[192,256]{1,0:T(8,128)(2,1)} %param.8) | copy-start | bytes 294916
  7.2 192.0 %all-gather.3.cloned.1.call-start = ((), (), s32[]{:S(2)}) async-start(), calls=%async_computation.1 | async-start | bytes 6389760 | tf_op jit(solution)/shard_map/all_gather | solution.py:72
  7.9 368.0 %all-gather.5.cloned.1.call-start = ((), (), s32[]{:S(2)}) async-start(), calls=%async_computation.2 | async-start | bytes 6389760 | tf_op jit(solution)/shard_map/all_gather | solution.py:73
  10.9 7.6 %copy-start.2 = (s32[3,2]{0,1:T(2,128)S(1)}, s32[3,2]{0,1:T(2,128)}, u32[]{:S(2)}) copy-start(s32[3,2]{0,1:T(2,128)} %param.13) | copy-start | bytes 76
  10.9 7.8 %copy-start.1 = (bf16[192,256]{1,0:T(8,128)(2,1)S(1)}, bf16[192,256]{1,0:T(8,128)(2,1)}, u32[]{:S(2)}) copy-start(bf16[192,256]{1,0:T(8,128)(2,1)} %param.11) | copy-start | bytes 294916
  10.9 34.5 %all-to-all-start = ((bf16[1,128,8,512]{1,3,0,2:T(8,128)(2,1)}), bf16[1,128,8,512]{1,3,0,2:T(8,128)(2,1)S(1)}, u32[]{:S(2)}, u32[]{:S(2)}) async-start(bf16[1,128,8,512]{1,3,0,2:T(8,128)(2,1)} %bitcast.1), calls=%async_computation | async-start | bytes 2097152 | tf_op jit(solution)/shard_map/all_to_all | solution.py:91
Sparse Core Ops, SparseCore 0:
  12.4 186.6 all-gather.2
  203.6 172.2 all-gather.4
where the time goes:
time: 455 us; the launch traced here: 454 us
  waiting for transfers between devices  346 us (76%)
  local copies, waits for them, and re-layouts  53.5 us (12%)
  matrix products  14.5 us (3%)
  between operations  14.2 us (3%)
  other arithmetic  11.1 us (2%)
  loops' own time  7.49 us (2%)
  starting transfers between devices  7.47 us (2%)
    all_gather x1, waiting for transfers between devices, self_attention(): lax.all_gather(value_self, 'ctx', axis=0, tiled=True)  167 us
    all_gather x1, waiting for transfers between devices, self_attention(): lax.all_gather(key_self, 'ctx', axis=0, tiled=True)  151 us
    dynamic_slice x24, local copies, waits for them, and re-layouts, attend_keys(): lax.scan(fold_step, carried, (jnp.arange(blocks, dtype=jnp.int32), key_st...  29.8 us
    all_to_all x1, waiting for transfers between devices, cross_attention(): lax.all_to_all(parted, ('sec', 'head'), split_axis=2, concat_axis=0, tile...  26.6 us
    reshape x1, local copies, waits for them, and re-layouts, attend_keys(): value_stack = value_rows.reshape(blocks, block_rows, head_count, HD)  9.73 us
    reshape x1, local copies, waits for them, and re-layouts, attend_keys(): key_stack = key_rows.reshape(blocks, block_rows, head_count, HD)  9.69 us
  transfers between devices with their start and end apart: 3, of which 3 were waited for; matrix products, arithmetic and copies ran while one was open for 3% of the time, Pallas kernels for 0%

commit v1 on v0

--- a/solution.py
+++ b/solution.py
@@ -7,6 +7,13 @@
 HD = 128
 STRETCH = 64
 MASKED_SCORE = -1e30
+
+
+def swapped_in(block, axis, d):
+    devices = lax.axis_size(axis)
+    pieces = jnp.stack([block for _ in range(devices)])
+    pieces = lax.all_to_all(pieces, axis, split_axis=0, concat_axis=0)
+    return jnp.concatenate(pieces, axis=d)
 
 
 def attend_block(carried, queries, key_block, value_block, key_mask, score_scale):
@@ -70,7 +77,7 @@
         carried,
         queries,
         lax.all_gather(key_self, "ctx", axis=0, tiled=True),
-        lax.all_gather(value_self, "ctx", axis=0, tiled=True),
+        swapped_in(value_self, "ctx", 0),
         positions,
         score_scale,
     )

time: 455 us -> 423 us (0.930)
  waiting for transfers between devices: 346 us -> 267 us
  blocking collectives: 0 us -> 33.4 us
  starting transfers between devices: 7.47 us -> 16.8 us
    all_gather x1 -> x0, waiting for transfers between devices: 167 us -> none  [self_attention(): lax.all_gather(value_self, 'ctx', axis=0, tiled=True)]
    all_to_all x1, waiting for transfers between devices: 26.6 us -> 146 us  [swapped_in(): pieces = lax.all_to_all(pieces, axis, split_axis=0, concat_axis=0)]
    all_to_all x0 -> x1, blocking collectives: none -> 33.4 us  [cross_attention(): lax.all_to_all(parted, ('sec', 'head'), split_axis=2, concat_axis=0, tile...]
    all_gather x1, waiting for transfers between devices: 151 us -> 121 us  [self_attention(): lax.all_gather(key_self, 'ctx', axis=0, tiled=True)]
    another operation x0 -> x2, local copies, waits for them, and re-layouts: none -> 13.2 us  [the longest x1 9.78 us: attend_keys(): value_stack = value_rows.reshape(blocks, block_rows, head_count, HD)]
    reshape x1 -> x0, local copies, waits for them, and re-layouts: 9.73 us -> none  [attend_keys(): value_stack = value_rows.reshape(blocks, block_rows, head_count, HD)]
    all_to_all x1, starting transfers between devices: 7.4 us -> 16.8 us  [swapped_in(): pieces = lax.all_to_all(pieces, axis, split_axis=0, concat_axis=0)]
  transfers between devices with their start and end apart: 3 -> 2, of which waited for: 3 -> 2; matrix products, arithmetic and copies ran while one was open for 3% -> 3% of each run, Pallas kernels for 0% -> 0%
where the time goes in v1:
time: 423 us; the launch traced here: 422 us
  waiting for transfers between devices  267 us (63%)
  local copies, waits for them, and re-layouts  57.1 us (13%)
  blocking collectives  33.4 us (8%)
  starting transfers between devices  16.8 us (4%)
  matrix products  14.2 us (3%)
  between operations  14.2 us (3%)
  other arithmetic  10.9 us (3%)
  loops' own time  8.51 us (2%)
    all_to_all x1, waiting for transfers between devices, swapped_in(): pieces = lax.all_to_all(pieces, axis, split_axis=0, concat_axis=0)  146 us
    all_gather x1, waiting for transfers between devices, self_attention(): lax.all_gather(key_self, 'ctx', axis=0, tiled=True)  121 us
    all_to_all x1, blocking collectives, cross_attention(): lax.all_to_all(parted, ('sec', 'head'), split_axis=2, concat_axis=0, tile...  33.4 us
    dynamic_slice x24, local copies, waits for them, and re-layouts, attend_keys(): lax.scan(fold_step, carried, (jnp.arange(blocks, dtype=jnp.int32), key_st...  30.6 us
    all_to_all x1, starting transfers between devices, swapped_in(): pieces = lax.all_to_all(pieces, axis, split_axis=0, concat_axis=0)  16.8 us
    another operation x1, local copies, waits for them, and re-layouts, attend_keys(): value_stack = value_rows.reshape(blocks, block_rows, head_count, HD)  9.78 us
    reshape x1, local copies, waits for them, and re-layouts, attend_keys(): key_stack = key_rows.reshape(blocks, block_rows, head_count, HD)  9.72 us
    another operation x1, loops' own time, attend_keys(): lax.scan(fold_step, carried, (jnp.arange(blocks, dtype=jnp.int32), key_st...  8.51 us
  transfers between devices with their start and end apart: 2, of which 2 were waited for; matrix products, arithmetic and copies ran while one was open for 3% of the time, Pallas kernels for 0%

profile of v1, /device:TPU:4, one launch (start us, length us, event | category | flops | bytes accessed | tf_op | source)
XLA Modules:
  0.0 422.3 jit_solution(8643528946486859085)
XLA Ops:
  7.2 1.6 copy.37
  8.8 33.4 %all_to_all.20 = bf16[1,128,8,512]{1,3,0,2:T(8,128)(2,1)S(1)} all-to-all(bf16[1,128,8,512]{1,3,0,2:T(8,128)(2,1)S(1)} %bitcast.70), channel_id=1, replica_groups=mesh['sec'=2,'ctx'=64,'head'=4] {'sec','head'}, dimensions={2} | all-to-all | bytes 2097152 | tf_op jit(solution)/shard_map/all_to_all | solution.py:98
  42.3 3.4 stack.2
  45.7 16.8 %all-to-all-start = ((bf16[64,192,256]{2,1,0:T(8,128)(2,1)}), bf16[64,192,256]{2,1,0:T(8,128)(2,1)}, u32[]{:S(2)}, u32[]{:S(2)}) async-start(bf16[64,192,256]{2,1,0:T(8,128)(2,1)} %stack.2), calls=%async_computation | async-start | bytes 12582912 | tf_op jit(solution)/shard_map/all_to_all | solution.py:15
  62.5 0.7 all-gather.2.cloned.1.call-update
  63.6 0.7 copy.39
  64.3 0.7 gather_fusion
  66.1 0.7 fusion.18
  66.8 145.7 %all-to-all-done = bf16[64,192,256]{2,1,0:T(8,128)(2,1)} async-done(((bf16[64,192,256]{2,1,0:T(8,128)(2,1)}), bf16[64,192,256]{2,1,0:T(8,128)(2,1)}, u32[]{:S(2)}, u32[]{:S(2)}) %all-to-all-start) | async-done | bytes 6291488 | tf_op jit(solution)/shard_map/all_to_all | solution.py:15
  212.5 9.8 %reshape_reshape.3 = bf16[12,1024,2,128]{3,2,1,0:T(2,128)(2,1)} reshape(bf16[64,192,256]{2,1,0:T(8,128)(2,1)} %all-to-all-done) | data formatting | bytes 12582912 | tf_op jit(solution)/shard_map/reshape;reshape | solution.py:46
  222.3 120.8 %all-gather.2.cloned.1.call-done = bf16[12288,256]{1,0:T(8,128)(2,1)} async-done(((bf16[192,256]{1,0:T(8,128)(2,1)}), bf16[12288,256]{1,0:T(8,128)(2,1)}) %all-gather.2.cloned.1.call-update) | async-done | bytes 6291472 | tf_op jit(solution)/shard_map/all_gather | solution.py:79
  343.1 9.7 %reshape.95 = bf16[12,1024,2,128]{3,2,1,0:T(2,128)(2,1)} reshape(bf16[12288,256]{1,0:T(8,128)(2,1)} %all-gather.2.cloned.1.call-done) | data formatting | bytes 12582912 | tf_op jit(solution)/shard_map/reshape | solution.py:45
  352.8 61.8 %while.15 = (s32[]{:T(128)}, f32[2,192]{1,0:T(2,128)S(1)}, f32[2,192]{1,0:T(2,128)S(1)}, f32[192,2,128]{2,0,1:T(8,128)S(1)}, s32[12]{0:T(128)S(1)}, /*index=5*/b...) while((s32[]{:T(128)}, f32[2,192]{1,0:T(2,128)S(1)}, ...), condition=%wide.region_3.4_spmd.clone, body=%wide.region_0.3_spmd.clone.sunk | while | flops 205411776 | bytes 9178793 | solution.py:59
  354.3 1.9 constant_dynamic-slice_fusion.3
  358.0 0.6 dynamic_slice.19
  359.5 1.9 constant_dynamic-slice_fusion.3
  363.1 0.6 dynamic_slice.19
  364.6 1.9 constant_dynamic-slice_fusion.3
  368.3 0.6 dynamic_slice.19
  369.8 1.9 constant_dynamic-slice_fusion.3
  373.4 0.6 dynamic_slice.19
  374.9 1.9 constant_dynamic-slice_fusion.3
  378.6 0.6 dynamic_slice.19
  380.1 1.9 constant_dynamic-slice_fusion.3
  383.8 0.6 dynamic_slice.19
  385.3 1.9 constant_dynamic-slice_fusion.3
  390.4 1.9 constant_dynamic-slice_fusion.3
  395.6 1.9 constant_dynamic-slice_fusion.3
  400.7 1.9 constant_dynamic-slice_fusion.3
  405.9 1.9 constant_dynamic-slice_fusion.3
  411.0 1.9 constant_dynamic-slice_fusion.3
  414.7 0.8 copy_bitcast_fusion.8
  (154 shorter events, 28.0 us)
Async XLA Ops:
  7.2 56.5 %copy-start = (bf16[192,256]{1,0:T(8,128)(2,1)S(1)}, bf16[192,256]{1,0:T(8,128)(2,1)}, u32[]{:S(2)}) copy-start(bf16[192,256]{1,0:T(8,128)(2,1)} %param.8) | copy-start | bytes 294916
  8.8 33.4 %copy-start.2 = (bf16[192,256]{1,0:T(8,128)(2,1)S(1)}, bf16[192,256]{1,0:T(8,128)(2,1)}, u32[]{:S(2)}) copy-start(bf16[192,256]{1,0:T(8,128)(2,1)} %param.10) | copy-start | bytes 294916
  45.7 17.5 %copy-start.3 = (s32[3,2]{0,1:T(2,128)S(1)}, s32[3,2]{0,1:T(2,128)}, u32[]{:S(2)}) copy-start(s32[3,2]{0,1:T(2,128)} %param.13) | copy-start | bytes 76
  45.7 17.7 %copy-start.1 = (bf16[192,256]{1,0:T(8,128)(2,1)S(1)}, bf16[192,256]{1,0:T(8,128)(2,1)}, u32[]{:S(2)}) copy-start(bf16[192,256]{1,0:T(8,128)(2,1)} %param.11) | copy-start | bytes 294916
  45.7 166.9 %all-to-all-start = ((bf16[64,192,256]{2,1,0:T(8,128)(2,1)}), bf16[64,192,256]{2,1,0:T(8,128)(2,1)}, u32[]{:S(2)}, u32[]{:S(2)}) async-start(bf16[64,192,256]{2,1,0:T(8,128)(2,1)} %stack.2), calls=%async_computation | async-start | bytes 12582912 | tf_op jit(solution)/shard_map/all_to_all | solution.py:15
  62.4 280.7 %all-gather.2.cloned.1.call-start = ((), (), s32[]{:S(2)}) async-start(), calls=%async_computation.2 | async-start | bytes 6389760 | tf_op jit(solution)/shard_map/all_gather | solution.py:79
Sparse Core Ops, SparseCore 0:
  67.7 275.3 all-gather.1
